TPU v7x, 32 devices: a whole 2x2x4 slice. The times are simulated.
32 devices in a mesh: tm: 2 (over x), row: 4 (over z), col: 4 (over y, core).
Axes of the slice: x: 2, y: 2, z: 4, core: 2. Of those that a mesh axis runs over, the one named last changes fastest.
Arguments:
- features: bfloat16 [4, 60, 104, 128], P('tm', 'row', 'col'), may hold values from -13 to 13
- cotangent: bfloat16 [4, 60, 104, 128], P('tm', 'row', 'col'), may hold values from -7 to 7
- conv_one: bfloat16 [27, 128, 128], replicated, may hold values from -0.109375 to 0.109375
- conv_two: bfloat16 [27, 128, 128], replicated, may hold values from -0.109375 to 0.109375
- gain_one: float32 [128], replicated, may hold values from 0.25 to 1.75
- shift_one: float32 [128], replicated, may hold values from -0.6 to 0.6
- gain_two: float32 [128], replicated, may hold values from 0.25 to 1.75
- shift_two: float32 [128], replicated, may hold values from -0.6 to 0.6
Outputs:
- block_out: bfloat16 [4, 60, 104, 128], P('tm', 'row', 'col')
- grad_input: bfloat16 [4, 60, 104, 128], P('tm', 'row', 'col')
- grad_conv_one: float32 [27, 128, 128], replicated
- grad_conv_two: float32 [27, 128, 128], replicated
All inputs are finite; a program needn't handle non-finite values.
Results may differ from a plain program's by a relative error of at most 0.0034.
Values may be sent and summed in bfloat16 or wider, within the bound.
A program may use at most 128 MiB of HBM per device.

v0:
```python
import jax
import jax.numpy as jnp
from jax import lax
from jax.sharding import PartitionSpec as P

GROUPS = 32


epsilon = 1e-05


def passed_along(value, axis, steps):
    count = lax.axis_size(axis)
    leading, last = (max(0, -steps), min(count, count - steps))
    return lax.ppermute(value, axis, [(source, source + steps) for source in range(leading, last)])


def with_halo(block, sides, width):
    for axis, dim in sides:
        count = lax.axis_size(axis)
        forward = [(i, i + 1) for i in range(count - 1)]
        backward = [(target, source) for source, target in forward]
        low = lax.ppermute(
            lax.slice_in_dim(block, block.shape[dim] - width, None, axis=dim), axis, forward
        )
        high = lax.ppermute(lax.slice_in_dim(block, 0, width, axis=dim), axis, backward)
        block = jnp.concatenate([low, block, high], axis=dim)
    return block


def unfold_taps(padded, frames, height, width):
    pieces = []
    for frame_off in range(3):
        for row_off in range(3):
            for col_off in range(3):
                pieces.append(
                    padded[
                        frame_off : frame_off + frames,
                        row_off : row_off + height,
                        col_off : col_off + width,
                    ]
                )
    stacked = jnp.concatenate(pieces, axis=3)
    return stacked.reshape(frames * height * width, stacked.shape[3])


def extend_past(activation):
    carried = passed_along(activation, "tm", 1)
    joined = jnp.concatenate([carried, activation], axis=0)
    return with_halo(joined, (("row", 1), ("col", 2)), 1)


def extend_future(gradient):
    carried = passed_along(gradient, "tm", -1)
    joined = jnp.concatenate([gradient, carried], axis=0)
    return with_halo(joined, (("row", 1), ("col", 2)), 1)


def group_moments(values, members):
    channels = values.shape[3]
    per_group = channels // GROUPS
    grouped = values.reshape(-1, GROUPS, per_group)
    summed, squares = lax.psum(
        (jnp.sum(grouped, axis=(0, 2)), jnp.sum(grouped * grouped, axis=(0, 2))),
        ("tm", "row", "col"),
    )
    average = summed / members
    variance = squares / members - average * average
    return (jnp.repeat(average, per_group), jnp.repeat(lax.rsqrt(variance + epsilon), per_group))


def group_backward(lifted, unit, members, weight_part):
    channels = lifted.shape[3]
    per_group = channels // GROUPS
    first = jnp.sum(lifted.reshape(-1, GROUPS, per_group), axis=(0, 2))
    second = jnp.sum((lifted * unit).reshape(-1, GROUPS, per_group), axis=(0, 2))
    first, second = lax.psum((first, second), ("tm", "row", "col"))
    return (
        jnp.repeat(first / members, per_group),
        jnp.repeat(second / members, per_group),
        weight_part,
    )


def silu_slope(normed):
    sigm = jax.nn.sigmoid(normed)
    return sigm * (1.0 + normed * (1.0 - sigm))


def kernel_term(columns, gradient_flat, kernel_shape):
    term = lax.dot_general(
        columns, gradient_flat, (((0,), (0,)), ((), ())), preferred_element_type=jnp.float32
    )
    return term.reshape(kernel_shape)


def local(features, cotangent, conv_one, conv_two, gain_one, shift_one, gain_two, shift_two):
    frames, height, width, channels = features.shape
    voxels = frames * height * width
    kernel_rows = conv_one.shape[0] * channels
    members = float(
        voxels
        * lax.axis_size("tm")
        * lax.axis_size("row")
        * lax.axis_size("col")
        * (channels // GROUPS)
    )
    inputs_wide = features.astype(jnp.float32)
    average_one, scale_one = group_moments(inputs_wide, members)
    unit_one = (inputs_wide - average_one) * scale_one
    normed_one = unit_one * gain_one + shift_one
    acted_one = jax.nn.silu(normed_one).astype(jnp.bfloat16)
    columns_one = unfold_taps(extend_past(acted_one), frames, height, width)
    hidden = jnp.dot(
        columns_one, conv_one.reshape(kernel_rows, channels), preferred_element_type=jnp.float32
    )
    hidden = hidden.reshape(frames, height, width, channels)
    average_two, scale_two = group_moments(hidden, members)
    unit_two = (hidden - average_two) * scale_two
    normed_two = unit_two * gain_two + shift_two
    acted_two = jax.nn.silu(normed_two).astype(jnp.bfloat16)
    columns_two = unfold_taps(extend_past(acted_two), frames, height, width)
    branch_out = jnp.dot(
        columns_two, conv_two.reshape(kernel_rows, channels), preferred_element_type=jnp.float32
    )
    block_out = (inputs_wide + branch_out.reshape(frames, height, width, channels)).astype(
        jnp.bfloat16
    )
    part_two = kernel_term(columns_two, cotangent.reshape(voxels, channels), conv_two.shape)
    back_columns = unfold_taps(extend_future(cotangent), frames, height, width)
    flip_two = jnp.flip(conv_two, 0).transpose(0, 2, 1).reshape(kernel_rows, channels)
    back_two = jnp.dot(back_columns, flip_two, preferred_element_type=jnp.float32).reshape(
        frames, height, width, channels
    )
    lifted_two = back_two * silu_slope(normed_two) * gain_two
    mean_first, mean_second, sum_two = group_backward(lifted_two, unit_two, members, part_two)
    grad_hidden = (scale_two * (lifted_two - mean_first - unit_two * mean_second)).astype(
        jnp.bfloat16
    )
    part_one = kernel_term(columns_one, grad_hidden.reshape(voxels, channels), conv_one.shape)
    hidden_columns = unfold_taps(extend_future(grad_hidden), frames, height, width)
    flip_one = jnp.flip(conv_one, 0).transpose(0, 2, 1).reshape(kernel_rows, channels)
    back_one = jnp.dot(hidden_columns, flip_one, preferred_element_type=jnp.float32).reshape(
        frames, height, width, channels
    )
    lifted_one = back_one * silu_slope(normed_one) * gain_one
    mean_first, mean_second, sum_one = group_backward(lifted_one, unit_one, members, part_one)
    grad_input = (
        cotangent.astype(jnp.float32)
        + scale_one * (lifted_one - mean_first - unit_one * mean_second)
    ).astype(jnp.bfloat16)
    sum_two, sum_one = lax.psum((sum_two, sum_one), ("tm", "row", "col"))
    return (block_out, grad_input, sum_one, sum_two)


def solution(mesh):
    return jax.shard_map(
        local,
        mesh=mesh,
        in_specs=(
            P("tm", "row", "col", None),
            P("tm", "row", "col", None),
            P(),
            P(),
            P(),
            P(),
            P(),
            P(),
        ),
        out_specs=(P("tm", "row", "col", None), P("tm", "row", "col", None), P(), P()),
        check_vma=False,
    )
```

profile of v0, /device:TPU:0, one launch (start us, length us, event | category | flops | bytes accessed | tf_op | source)
XLA Modules:
  0.0 459.8 jit_solution(12720867220657002777)
XLA Ops:
  8.7 42.0 %all-reduce.3 = (f32[32]{0:T(128)S(1)}, f32[32]{0:T(128)S(1)}) all-reduce(f32[32]{0:T(128)S(1)} %reduce_sum.100, f32[32]{0:T(128)S(1)} %reduce_sum.97), channel_id=1, replica_groups=mesh['tm'=2,'row'=4,'col'=4] {'tm','row','col'}, use_global_device_ids=true, to_apply=%region_5.6 | all-reduce | flops 64 | bytes 512 | tf_op jit(solution)/shard_map/psum | solution.py:63
  52.3 4.2 collective-permute-start
  59.5 1.9 copy.25
  61.4 1.9 copy.24
  64.3 3.4 collective-permute-start.1
  69.1 4.5 collective-permute-start.11
  76.4 3.0 collective-permute-start.3
  79.6 1.3 collective-permute-start.14
  102.4 8.2 %reshape.75 = bf16[780,3456]{1,0:T(8,128)(2,1)} reshape(bf16[2,15,26,3456]{3,2,1,0:T(8,128)(2,1)} %slice_dynamic-update-slice_fusion.67) | data formatting | bytes 10782720 | tf_op jit(solution)/shard_map/reshape | solution.py:44
  110.7 4.2 fusion.42
  115.3 3.0 collective-permute-start.13
  118.4 42.4 %all-reduce.2 = (f32[32]{0:T(128)S(1)}, f32[32]{0:T(128)S(1)}) all-reduce(f32[32]{0:T(128)S(1)} %reduce_sum.112, f32[32]{0:T(128)S(1)} %reduce_sum.106), channel_id=1, replica_groups=mesh['tm'=2,'row'=4,'col'=4] {'tm','row','col'}, use_global_device_ids=true, to_apply=%region_11.12 | all-reduce | flops 64 | bytes 512 | tf_op jit(solution)/shard_map/psum | solution.py:63
  164.0 2.8 fusion.41
  167.3 39.2 %all-reduce.1 = (f32[32]{0:T(128)S(1)}, f32[32]{0:T(128)S(1)}) all-reduce(f32[32]{0:T(128)S(1)} %reduce_sum.145, f32[32]{0:T(128)S(1)} %reduce_sum.115), channel_id=1, replica_groups=mesh['tm'=2,'row'=4,'col'=4] {'tm','row','col'}, use_global_device_ids=true, to_apply=%region_17.18 | all-reduce | flops 64 | bytes 512 | tf_op jit(solution)/shard_map/psum | solution.py:77
  206.9 1.3 multiply_convert_fusion
  209.6 10.0 %dot_general.31 = bf16[27,128,780]{1,0,2:T(8,128)(2,1)} reshape(bf16[3456,780]{0,1:T(8,128)(2,1)} %bitcast.36) | data formatting | bytes 10782720 | tf_op jit(solution)/shard_map/dot_general | solution.py:91
  219.6 4.6 collective-permute-start.5
  224.2 9.4 %fusion.2 = f32[27,128,128]{2,1,0:T(8,128)} fusion(bf16[780,128,1]{1,0,2:T(8,128)(2,1)S(1)} %reshape.87, bf16[27,128,780]{1,0,2:T(8,128)(2,1)} %dot_general.31), kind=kOutput, calls=%fused_computation.2 | convolution fusion | flops 690094080 | bytes 7360512 | tf_op jit(solution)/shard_map/dot_general | solution.py:91
  233.6 3.5 collective-permute-start.6
  238.5 4.5 collective-permute-start.16
  245.7 3.0 collective-permute-start.8
  250.2 4.4 collective-permute-start.18
  276.1 8.2 %reshape.82 = bf16[780,3456]{1,0:T(8,128)(2,1)} reshape(bf16[2,15,26,3456]{3,2,1,0:T(8,128)(2,1)} %slice_dynamic-update-slice_fusion.43) | data formatting | bytes 10782720 | tf_op jit(solution)/shard_map/reshape | solution.py:44
  284.3 10.0 %dot_general.34 = bf16[27,128,780]{1,0,2:T(8,128)(2,1)} reshape(bf16[3456,780]{0,1:T(8,128)(2,1)} %bitcast.37) | data formatting | bytes 10782720 | tf_op jit(solution)/shard_map/dot_general | solution.py:91
  297.1 2.7 copy-done.6
  299.8 6.8 %fusion = f32[27,128,128]{2,1,0:T(8,128)} fusion(bf16[780,128,1]{1,0,2:T(8,128)(2,1)S(1)} %copy-done.5, bf16[27,128,780]{1,0,2:T(8,128)(2,1)S(1)} %bitcast.39), kind=kOutput, calls=%fused_computation | convolution fusion | flops 690094080 | bytes 7360512 | tf_op jit(solution)/shard_map/dot_general | solution.py:91
  306.7 5.0 %fusion.40 = (f32[128]{0:T(128)S(1)}, f32[128]{0:T(128)S(1)}, f32[2,15,26,128]{3,2,1,0:T(8,128)S(1)}) fusion(f32[128]{0:T(128)S(1)} %mul.127, f32[128]{0:T(128)S(1)} %sub.58, bf16[2,15,26,128]{3,0,2,1:T(2,128)(2,1)S(1)} %copy-done, f32[128]{0:T(128)S(1)} %copy-done.7, f32[128]{0:T(128)S(1)} %copy-done.8, bf16[2,15,26,3456]{3,2,1,0:T(8,128)(2,1)} %copy-done.6, ...), kind=kOutput, calls=%fused_computation.210 | convolution fusion | flops 691791104 | bytes 6878208 | tf_op jit(solution)/shard_map/dot_general | solution.py:143
  312.1 41.0 %all-reduce = (f32[32]{0:T(128)S(1)}, f32[32]{0:T(128)S(1)}) all-reduce(f32[32]{0:T(128)S(1)} %reduce_sum.151, f32[32]{0:T(128)S(1)} %reduce_sum.148), channel_id=1, replica_groups=mesh['tm'=2,'row'=4,'col'=4] {'tm','row','col'}, use_global_device_ids=true, to_apply=%region_23.24 | all-reduce | flops 64 | bytes 512 | tf_op jit(solution)/shard_map/psum | solution.py:77
  353.1 4.9 %fusion.6 = bf16[2,15,26,128]{3,2,1,0:T(8,128)(2,1)S(1)} fusion(bf16[2,15,26,3456]{3,2,1,0:T(8,128)(2,1)} %slice_dynamic-update-slice_fusion.43, bf16[3456,128,1,1]{1,0,3,2:T(8,128)(2,1)S(1)} %bitcast.41, bf16[2,15,26,128]{3,0,2,1:T(2,128)(2,1)S(1)} %copy-done), kind=kOutput, calls=%fused_computation.9 | convolution fusion | flops 690393600 | bytes 6675456 | tf_op jit(solution)/shard_map/dot_general | solution.py:123
  360.2 87.0 %all-reduce.7.cloned.1.call-done = (f32[27,128,128]{2,1,0:T(8,128)}, f32[27,128,128]{2,1,0:T(8,128)}) async-done(((f32[27,128,128]{2,1,0:T(8,128)}, f32[27,128,128]{2,1,0:T(8,128)}), (f32[27,128,128]{2,1,0:T(8,128)}, f32[27,128,128]{2,1,0:T(8,128)})) %all-reduce.7.cloned.1.call-update) | async-done | bytes 3538960 | tf_op jit(solution)/shard_map/psum | solution.py:152
  447.2 2.9 copy.158
  450.1 2.9 copy.159
  (229 shorter events, 70.4 us)
Async XLA Ops:
  7.2 440.1 %all-reduce.7.cloned.1.call-start = ((), (), s32[]{:S(2)}) async-start(), calls=%async_computation | async-start | bytes 7077888 | tf_op jit(solution)/shard_map/psum | solution.py:152
  52.3 12.0 %collective-permute-start = (bf16[2,15,26,128]{3,2,1,0:T(8,128)(2,1)S(1)}, bf16[2,15,26,128]{3,2,1,0:T(8,128)(2,1)S(1)}, u32[]{:S(2)}, u32[]{:S(2)}) collective-permute-start(bf16[2,15,26,128]{3,2,1,0:T(8,128)(2,1)S(1)} %fusion.18), channel_id=1, source_target_pairs={{0,16},{1,17},{2,18},{3,19},{4,20},{5,21},{6,22},{7,23},{8,24},{9,... | collective-permute-start | bytes 599048 | tf_op jit(solution)/shard_map/ppermute | solution.py:15
  57.5 11.6 %collective-permute-start.10 = (bf16[2,15,26,128]{3,2,1,0:T(8,128)(2,1)S(1)}, bf16[2,15,26,128]{3,2,1,0:T(8,128)(2,1)S(1)}, u32[]{:S(2)}, u32[]{:S(2)}) collective-permute-start(bf16[2,15,26,128]{3,2,1,0:T(8,128)(2,1)S(1)} %get-tuple-element.62), channel_id=1, source_target_pairs={{16,0},{17,1},{18,2},{19,3},{20,4},{21,5},{22,6},{23,7},{24,8},{25... | collective-permute-start | bytes 599048 | tf_op jit(solution)/shard_map/ppermute | solution.py:15
  64.3 10.6 %collective-permute-start.1 = (bf16[4,1,26,128]{3,2,1,0:T(8,128)(2,1)S(1)}, bf16[4,1,26,128]{3,2,1,0:T(8,128)(2,1)S(1)}, u32[]{:S(2)}, u32[]{:S(2)}) collective-permute-start(bf16[4,1,26,128]{3,2,1,0:T(8,128)(2,1)S(1)} %get-tuple-element.60), channel_id=1, source_target_pairs={{0,4},{4,8},{8,12},{1,5},{5,9},{9,13},{2,6},{6,10},{10,14},{3,7},{... | collective-permute-start | bytes 79880 | tf_op jit(solution)/shard_map/ppermute | solution.py:23
  67.7 7.2 %collective-permute-start.2 = (bf16[4,1,26,128]{3,2,1,0:T(8,128)(2,1)S(1)}, bf16[4,1,26,128]{3,2,1,0:T(8,128)(2,1)S(1)}, u32[]{:S(2)}, u32[]{:S(2)}) collective-permute-start(bf16[4,1,26,128]{3,2,1,0:T(8,128)(2,1)S(1)} %get-tuple-element.61), channel_id=1, source_target_pairs={{4,0},{8,4},{12,8},{5,1},{9,5},{13,9},{6,2},{10,6},{14,10},{7,3},{... | collective-permute-start | bytes 79880 | tf_op jit(solution)/shard_map/ppermute | solution.py:26
  69.1 10.3 %collective-permute-start.11 = (bf16[4,1,26,128]{3,2,1,0:T(8,128)(2,1)S(1)}, bf16[4,1,26,128]{3,2,1,0:T(8,128)(2,1)S(1)}, u32[]{:S(2)}, u32[]{:S(2)}) collective-permute-start(bf16[4,1,26,128]{3,2,1,0:T(8,128)(2,1)S(1)} %get-tuple-element.52), channel_id=1, source_target_pairs={{0,4},{4,8},{8,12},{1,5},{5,9},{9,13},{2,6},{6,10},{10,14},{3,7},{... | collective-permute-start | bytes 79880 | tf_op jit(solution)/shard_map/ppermute | solution.py:23
  73.7 5.8 %collective-permute-start.12 = (bf16[4,1,26,128]{3,2,1,0:T(8,128)(2,1)S(1)}, bf16[4,1,26,128]{3,2,1,0:T(8,128)(2,1)S(1)}, u32[]{:S(2)}, u32[]{:S(2)}) collective-permute-start(bf16[4,1,26,128]{3,2,1,0:T(8,128)(2,1)S(1)} %get-tuple-element.53), channel_id=1, source_target_pairs={{4,0},{8,4},{12,8},{5,1},{9,5},{13,9},{6,2},{10,6},{14,10},{7,3},{... | collective-permute-start | bytes 79880 | tf_op jit(solution)/shard_map/ppermute | solution.py:26
  75.1 5.9 %collective-permute-start.4 = (bf16[4,17,1,128]{3,2,1,0:T(2,128)(2,1)S(1)}, bf16[4,17,1,128]{3,2,1,0:T(2,128)(2,1)S(1)}, u32[]{:S(2)}, u32[]{:S(2)}) collective-permute-start(bf16[4,17,1,128]{3,2,1,0:T(2,128)(2,1)S(1)} %get-tuple-element.44), channel_id=1, source_target_pairs={{1,0},{2,1},{3,2},{5,4},{6,5},{7,6},{9,8},{10,9},{11,10},{13,12},{... | collective-permute-start | bytes 52232 | tf_op jit(solution)/shard_map/ppermute | solution.py:26
  76.4 4.7 %collective-permute-start.3 = (bf16[4,17,1,128]{3,2,1,0:T(2,128)(2,1)S(1)}, bf16[4,17,1,128]{3,2,1,0:T(2,128)(2,1)S(1)}, u32[]{:S(2)}, u32[]{:S(2)}) collective-permute-start(bf16[4,17,1,128]{3,2,1,0:T(2,128)(2,1)S(1)} %get-tuple-element.45), channel_id=1, source_target_pairs={{0,1},{1,2},{2,3},{4,5},{5,6},{6,7},{8,9},{9,10},{10,11},{12,13},{... | collective-permute-start | bytes 52232 | tf_op jit(solution)/shard_map/ppermute | solution.py:23
  79.6 81.6 %collective-permute-start.14 = (bf16[4,17,1,128]{3,2,1,0:T(2,128)(2,1)S(1)}, bf16[4,17,1,128]{3,2,1,0:T(2,128)(2,1)S(1)}, u32[]{:S(2)}, u32[]{:S(2)}) collective-permute-start(bf16[4,17,1,128]{3,2,1,0:T(2,128)(2,1)S(1)} %get-tuple-element.36), channel_id=1, source_target_pairs={{1,0},{2,1},{3,2},{5,4},{6,5},{7,6},{9,8},{10,9},{11,10},{13,12},{... | collective-permute-start | bytes 52232 | tf_op jit(solution)/shard_map/ppermute | solution.py:26
  81.0 17.4 %copy-start = (bf16[2,15,26,128]{3,0,2,1:T(2,128)(2,1)S(1)}, bf16[2,15,26,128]{3,0,2,1:T(2,128)(2,1)}, u32[]{:S(2)}) copy-start(bf16[2,15,26,128]{3,0,2,1:T(2,128)(2,1)} %param.8) | copy-start | bytes 599044
  81.0 17.4 %copy-start.7 = (f32[128]{0:T(128)S(1)}, f32[128]{0:T(128)}, u32[]{:S(2)}) copy-start(f32[128]{0:T(128)} %param.13) | copy-start | bytes 1540
  81.0 17.4 %copy-start.8 = (f32[128]{0:T(128)S(1)}, f32[128]{0:T(128)}, u32[]{:S(2)}) copy-start(f32[128]{0:T(128)} %param.12) | copy-start | bytes 1540
  100.9 9.8 %copy-start.2 = (bf16[27,128,128]{2,1,0:T(8,128)(2,1)S(1)}, bf16[27,128,128]{2,1,0:T(8,128)(2,1)}, u32[]{:S(2)}) copy-start(bf16[27,128,128]{2,1,0:T(8,128)(2,1)} %param.10) | copy-start | bytes 2654212
  110.7 51.3 %copy-start.1 = (bf16[2,15,26,128]{3,0,2,1:T(2,128)(2,1)S(1)}, bf16[2,15,26,128]{3,0,2,1:T(2,128)(2,1)}, u32[]{:S(2)}) copy-start(bf16[2,15,26,128]{3,0,2,1:T(2,128)(2,1)} %param.9) | copy-start | bytes 599044
  115.3 45.8 %collective-permute-start.13 = (bf16[4,17,1,128]{3,2,1,0:T(2,128)(2,1)S(1)}, bf16[4,17,1,128]{3,2,1,0:T(2,128)(2,1)S(1)}, u32[]{:S(2)}, u32[]{:S(2)}) collective-permute-start(bf16[4,17,1,128]{3,2,1,0:T(2,128)(2,1)S(1)} %get-tuple-element.37), channel_id=1, source_target_pairs={{0,1},{1,2},{2,3},{4,5},{5,6},{6,7},{8,9},{9,10},{10,11},{12,13},{... | collective-permute-start | bytes 52232 | tf_op jit(solution)/shard_map/ppermute | solution.py:23
  161.8 2.1 copy-start.4
  208.3 30.2 %collective-permute-start.15 = (bf16[2,15,26,128]{3,2,1,0:T(8,128)(2,1)S(1)}, bf16[2,15,26,128]{3,2,1,0:T(8,128)(2,1)S(1)}, u32[]{:S(2)}, u32[]{:S(2)}) collective-permute-start(bf16[2,15,26,128]{3,2,1,0:T(8,128)(2,1)S(1)} %get-tuple-element.46), channel_id=1, source_target_pairs={{16,0},{17,1},{18,2},{19,3},{20,4},{21,5},{22,6},{23,7},{24,8},{25... | collective-permute-start | bytes 599048 | tf_op jit(solution)/shard_map/ppermute | solution.py:15
  219.6 14.0 %collective-permute-start.5 = (bf16[2,15,26,128]{3,2,1,0:T(8,128)(2,1)S(1)}, bf16[2,15,26,128]{3,2,1,0:T(8,128)(2,1)S(1)}, u32[]{:S(2)}, u32[]{:S(2)}) collective-permute-start(bf16[2,15,26,128]{3,2,1,0:T(8,128)(2,1)S(1)} %get-tuple-element.47), channel_id=1, source_target_pairs={{0,16},{1,17},{2,18},{3,19},{4,20},{5,21},{6,22},{7,23},{8,24},{9,... | collective-permute-start | bytes 599048 | tf_op jit(solution)/shard_map/ppermute | solution.py:15
  233.6 10.7 %collective-permute-start.6 = (bf16[4,1,26,128]{3,2,1,0:T(8,128)(2,1)S(1)}, bf16[4,1,26,128]{3,2,1,0:T(8,128)(2,1)S(1)}, u32[]{:S(2)}, u32[]{:S(2)}) collective-permute-start(bf16[4,1,26,128]{3,2,1,0:T(8,128)(2,1)S(1)} %get-tuple-element.56), channel_id=1, source_target_pairs={{0,4},{4,8},{8,12},{1,5},{5,9},{9,13},{2,6},{6,10},{10,14},{3,7},{... | collective-permute-start | bytes 79880 | tf_op jit(solution)/shard_map/ppermute | solution.py:23
  237.1 7.2 %collective-permute-start.7 = (bf16[4,1,26,128]{3,2,1,0:T(8,128)(2,1)S(1)}, bf16[4,1,26,128]{3,2,1,0:T(8,128)(2,1)S(1)}, u32[]{:S(2)}, u32[]{:S(2)}) collective-permute-start(bf16[4,1,26,128]{3,2,1,0:T(8,128)(2,1)S(1)} %get-tuple-element.57), channel_id=1, source_target_pairs={{4,0},{8,4},{12,8},{5,1},{9,5},{13,9},{6,2},{10,6},{14,10},{7,3},{... | collective-permute-start | bytes 79880 | tf_op jit(solution)/shard_map/ppermute | solution.py:26
  238.5 10.3 %collective-permute-start.16 = (bf16[4,1,26,128]{3,2,1,0:T(8,128)(2,1)S(1)}, bf16[4,1,26,128]{3,2,1,0:T(8,128)(2,1)S(1)}, u32[]{:S(2)}, u32[]{:S(2)}) collective-permute-start(bf16[4,1,26,128]{3,2,1,0:T(8,128)(2,1)S(1)} %get-tuple-element.50), channel_id=1, source_target_pairs={{0,4},{4,8},{8,12},{1,5},{5,9},{9,13},{2,6},{6,10},{10,14},{3,7},{... | collective-permute-start | bytes 79880 | tf_op jit(solution)/shard_map/ppermute | solution.py:23
  243.0 5.8 %collective-permute-start.17 = (bf16[4,1,26,128]{3,2,1,0:T(8,128)(2,1)S(1)}, bf16[4,1,26,128]{3,2,1,0:T(8,128)(2,1)S(1)}, u32[]{:S(2)}, u32[]{:S(2)}) collective-permute-start(bf16[4,1,26,128]{3,2,1,0:T(8,128)(2,1)S(1)} %get-tuple-element.51), channel_id=1, source_target_pairs={{4,0},{8,4},{12,8},{5,1},{9,5},{13,9},{6,2},{10,6},{14,10},{7,3},{... | collective-permute-start | bytes 79880 | tf_op jit(solution)/shard_map/ppermute | solution.py:26
  244.4 10.4 %collective-permute-start.9 = (bf16[4,17,1,128]{3,2,1,0:T(2,128)(2,1)S(1)}, bf16[4,17,1,128]{3,2,1,0:T(2,128)(2,1)S(1)}, u32[]{:S(2)}, u32[]{:S(2)}) collective-permute-start(bf16[4,17,1,128]{3,2,1,0:T(2,128)(2,1)S(1)} %get-tuple-element.40), channel_id=1, source_target_pairs={{1,0},{2,1},{3,2},{5,4},{6,5},{7,6},{9,8},{10,9},{11,10},{13,12},{... | collective-permute-start | bytes 52232 | tf_op jit(solution)/shard_map/ppermute | solution.py:26
  245.7 9.1 %collective-permute-start.8 = (bf16[4,17,1,128]{3,2,1,0:T(2,128)(2,1)S(1)}, bf16[4,17,1,128]{3,2,1,0:T(2,128)(2,1)S(1)}, u32[]{:S(2)}, u32[]{:S(2)}) collective-permute-start(bf16[4,17,1,128]{3,2,1,0:T(2,128)(2,1)S(1)} %get-tuple-element.41), channel_id=1, source_target_pairs={{0,1},{1,2},{2,3},{4,5},{5,6},{6,7},{8,9},{9,10},{10,11},{12,13},{... | collective-permute-start | bytes 52232 | tf_op jit(solution)/shard_map/ppermute | solution.py:23
  248.9 45.5 %collective-permute-start.19 = (bf16[4,17,1,128]{3,2,1,0:T(2,128)(2,1)S(1)}, bf16[4,17,1,128]{3,2,1,0:T(2,128)(2,1)S(1)}, u32[]{:S(2)}, u32[]{:S(2)}) collective-permute-start(bf16[4,17,1,128]{3,2,1,0:T(2,128)(2,1)S(1)} %get-tuple-element.32), channel_id=1, source_target_pairs={{1,0},{2,1},{3,2},{5,4},{6,5},{7,6},{9,8},{10,9},{11,10},{13,12},{... | collective-permute-start | bytes 52232 | tf_op jit(solution)/shard_map/ppermute | solution.py:26
  250.2 44.2 %collective-permute-start.18 = (bf16[4,17,1,128]{3,2,1,0:T(2,128)(2,1)S(1)}, bf16[4,17,1,128]{3,2,1,0:T(2,128)(2,1)S(1)}, u32[]{:S(2)}, u32[]{:S(2)}) collective-permute-start(bf16[4,17,1,128]{3,2,1,0:T(2,128)(2,1)S(1)} %get-tuple-element.33), channel_id=1, source_target_pairs={{0,1},{1,2},{2,3},{4,5},{5,6},{6,7},{8,9},{9,10},{10,11},{12,13},{... | collective-permute-start | bytes 52232 | tf_op jit(solution)/shard_map/ppermute | solution.py:23
  294.4 5.5 %slice-start = ((s8[6389760]{0:T(1024)(128)(4,1)}), s8[4194304]{0:T(1024)(128)(4,1)S(1)}, s32[]{:S(2)}) async-start(s8[6389760]{0:T(1024)(128)(4,1)} %bitcast.38), calls=%async_computation.1 | async-start | bytes 8388608
  294.9 5.0 %copy-start.5 = (bf16[780,128,1]{1,0,2:T(8,128)(2,1)S(1)}, bf16[780,128,1]{1,0,2:T(8,128)(2,1)}, u32[]{:S(2)}) copy-start(bf16[780,128,1]{1,0,2:T(8,128)(2,1)} %reshape.88) | copy-start | bytes 599044
  295.7 4.1 slice-start.1
  297.1 2.8 copy-start.6
  306.7 46.5 %copy-start.3 = (bf16[27,128,128]{2,1,0:T(8,128)(2,1)S(1)}, bf16[27,128,128]{2,1,0:T(8,128)(2,1)}, u32[]{:S(2)}) copy-start(bf16[27,128,128]{2,1,0:T(8,128)(2,1)} %param.11) | copy-start | bytes 2654212
  (2 other events, 4.2 us)
Sparse Core Ops, SparseCore 0:
  306.8 140.4 all-reduce.6
where the time goes:
time: 462 us; the launch traced here: 460 us
  blocking collectives  165 us (36%)
  local copies, waits for them, and re-layouts  98.6 us (21%)
  waiting for transfers between devices  87.2 us (19%)
  starting transfers between devices  51.2 us (11%)
  matrix products  33 us (7%)
  between operations  15.1 us (3%)
  other arithmetic  10 us (2%)
    psum x1, waiting for transfers between devices, local(): sum_two, sum_one = lax.psum((sum_two, sum_one), ('tm', 'row', 'col'))  87 us
    psum x2, blocking collectives, group_moments(): lax.psum((jnp.sum(grouped, axis=(0, 2)), jnp.sum(grouped * grouped, axis=...  84.4 us
    psum x2, blocking collectives, group_backward(): first, second = lax.psum((first, second), ('tm', 'row', 'col'))  80.3 us
    unnamed x127, local copies, waits for them, and re-layouts  56.1 us
    ppermute x8, starting transfers between devices, with_halo(): lax.ppermute(lax.slice_in_dim(block, block.shape[dim] - width, None, axis...  29.5 us
    dot_general x2, local copies, waits for them, and re-layouts, kernel_term(): lax.dot_general(columns, gradient_flat, (((0,), (0,)), ((), ())), preferr...  20.1 us
    reshape x2, local copies, waits for them, and re-layouts, unfold_taps(): return stacked.reshape(frames * height * width, stacked.shape[3])  16.5 us
    dot_general x2, matrix products, kernel_term(): lax.dot_general(columns, gradient_flat, (((0,), (0,)), ((), ())), preferr...  16.2 us
  transfers between devices with their start and end apart: 21, of which 3 were waited for; matrix products, arithmetic and copies ran while one was open for 25% of the time, Pallas kernels for 0%

commit v1 on v0

v1 whole, which is shorter than its diff:
```python
import functools

import jax
import jax.numpy as jnp
from jax import lax
from jax.experimental import pallas as pl
from jax.experimental.pallas import tpu as pltpu
from jax.sharding import PartitionSpec as P

GROUPS = 32
EPSILON = 1e-05
MESH = pl.DeviceIdType.MESH
F32 = jnp.float32
BF16 = jnp.bfloat16
AXES = ("tm", "row", "col")


class Plan:
    def __init__(self, f, h, w, c, sizes):
        self.f, self.h, self.w, self.c = f, h, w, c
        self.wp = 16
        while self.wp < w + 2:
            self.wp *= 2
        self.n = f * h * self.wp
        self.hp = h + 2
        self.np = (f + 2) * self.hp * self.wp
        self.cb = -(-(f * h) // 16) * 16
        self.rb = 2 * self.wp
        self.ntm, self.nrow, self.ncol = sizes
        self.na = self.nrow
        self.nb = self.ntm * self.ncol


class Link:
    def __init__(self, src, dst, sems, index, device, sends, receives):
        self.make = lambda: pltpu.make_async_remote_copy(
            src_ref=src,
            dst_ref=dst,
            send_sem=sems[0].at[index],
            recv_sem=sems[1].at[index],
            device_id=device,
            device_id_type=MESH,
        )
        self.sends, self.receives = sends, receives

    def start(self):
        if self.sends is None:
            self.make().start()
            return

        @pl.when(self.sends)
        def _():
            self.make().start()

    def wait_send(self):
        if self.sends is None:
            self.make().wait_send()
            return

        @pl.when(self.sends)
        def _():
            self.make().wait_send()

    def wait_recv(self):
        if self.receives is None:
            self.make().wait_recv()
            return

        @pl.when(self.receives)
        def _():
            self.make().wait_recv()


class Place:
    def __init__(self, plan):
        self.t, self.r, self.c = (lax.axis_index(a) for a in AXES)
        self.has = dict(
            left=self.c > 0,
            right=self.c < plan.ncol - 1,
            up=self.r > 0,
            down=self.r < plan.nrow - 1,
            past=self.t > 0,
            future=self.t < plan.ntm - 1,
        )
        self.dev = dict(
            left={"col": self.c - 1},
            right={"col": self.c + 1},
            up={"row": self.r - 1},
            down={"row": self.r + 1},
            past={"tm": self.t - 1},
            future={"tm": self.t + 1},
        )

    def partners(self, plan):
        rows = [{"row": lax.rem(self.r + d, plan.na)} for d in range(1, plan.na)]
        index = self.t * plan.ncol + self.c
        others = []
        for d in range(1, plan.nb):
            to = lax.rem(index + d, plan.nb)
            others.append({"tm": lax.div(to, plan.ncol), "col": lax.rem(to, plan.ncol)})
        return rows, others


class Reduce:
    def __init__(self, plan, place, refs, sems, base):
        self.own, self.slots_a, self.mid, self.slots_b = refs
        rows, others = place.partners(plan)
        self.a = [
            Link(self.own, self.slots_a.at[d], sems, base + d, dev, None, None)
            for d, dev in enumerate(rows)
        ]
        self.b = [
            Link(self.mid, self.slots_b.at[d], sems, base + len(rows) + d, dev, None, None)
            for d, dev in enumerate(others)
        ]

    def start(self, first, second):
        self.own[...] = jnp.zeros_like(self.own)
        self.own[0:1] = first
        self.own[1:2] = second
        for link in self.a:
            link.start()

    def middle(self):
        for link in self.a:
            link.wait_recv()
        total = self.own[...]
        for d in range(len(self.a)):
            total = total + self.slots_a[d]
        self.mid[...] = total
        for link in self.b:
            link.start()

    def finish(self):
        for link in self.b:
            link.wait_recv()
        total = self.mid[...]
        for d in range(len(self.b)):
            total = total + self.slots_b[d]
        return total

    def drain(self):
        for link in self.a + self.b:
            link.wait_send()


EX_SEMS = 10


class Exchange:
    def __init__(self, plan, place, refs, sems, base, directions):
        self.plan, self.place, self.directions = plan, place, directions
        self.own, self.cols_out, self.cols_in, self.rows_out, self.rows_in = refs[:5]
        has, dev = place.has, place.dev
        cb, half = plan.cb, plan.f * plan.wp
        self.cols = [
            Link(self.cols_out.at[pl.ds(0, cb)], self.cols_in.at[pl.ds(0, cb)], sems, base,
                 dev["left"], has["left"], has["right"]),
            Link(self.cols_out.at[pl.ds(cb, cb)], self.cols_in.at[pl.ds(cb, cb)], sems, base + 1,
                 dev["right"], has["right"], has["left"]),
        ]
        self.rows = [
            Link(self.rows_out.at[pl.ds(0, half)], self.rows_in.at[pl.ds(half, half)], sems,
                 base + 2, dev["up"], has["up"], has["down"]),
            Link(self.rows_out.at[pl.ds(half, half)], self.rows_in.at[pl.ds(0, half)], sems,
                 base + 3, dev["down"], has["down"], has["up"]),
        ]
        self.tm = {}
        for k, source in enumerate(directions):
            block, cols, rows = refs[5 + 3 * k : 8 + 3 * k]
            target = "future" if source == "past" else "past"
            links = [
                Link(src, dst, sems, base + 4 + 3 * k + j, dev[target], has[target], has[source])
                for j, (src, dst) in enumerate(
                    [(self.own, block), (self.cols_in, cols), (self.rows_in, rows)]
                )
            ]
            self.tm[source] = ((block, cols, rows), links)

    def clear(self):
        cb, half = self.plan.cb, self.plan.f * self.plan.wp
        has = self.place.has

        def zero(ref, part, cond):
            @pl.when(jnp.logical_not(cond))
            def _():
                ref[part] = jnp.zeros(ref.at[part].shape, ref.dtype)

        zero(self.cols_in, pl.ds(0, cb), has["right"])
        zero(self.cols_in, pl.ds(cb, cb), has["left"])
        zero(self.rows_in, pl.ds(0, half), has["up"])
        zero(self.rows_in, pl.ds(half, half), has["down"])
        for source, (refs, _) in self.tm.items():
            for ref in refs:
                zero(ref, pl.ds(0, ref.shape[0]), has[source])

    def start(self, wide, pick):
        self.own[...] = wide[...].astype(BF16)
        for source in self.directions:
            self.tm[source][1][0].start()
        self.cols_out[...] = jnp.dot(pick[...], self.own[...], preferred_element_type=F32).astype(BF16)
        for link in self.cols:
            link.start()

    def middle(self, wide, spread):
        plan = self.plan
        for link in self.cols:
            link.wait_recv()
        for source in self.directions:
            self.tm[source][1][1].start()
        self.wide_ext = wide
        ends = spread_cols(self.cols_in, spread)
        size = plan.h * plan.wp
        for f in range(plan.f):
            for k, at in enumerate((f * size, (f + 1) * size - plan.wp)):
                self.rows_out[pl.ds((k * plan.f + f) * plan.wp, plan.wp)] = (
                    wide[pl.ds(at, plan.wp)] + ends[at : at + plan.wp]
                ).astype(BF16)
        for link in self.rows:
            link.start()

    def later(self):
        for link in self.rows:
            link.wait_recv()
        for source in self.directions:
            self.tm[source][1][2].start()

    def finish(self):
        for source in self.directions:
            for link in self.tm[source][1]:
                link.wait_recv()

    def drain(self):
        for link in self.cols + self.rows:
            link.wait_send()
        for source in self.directions:
            for link in self.tm[source][1]:
                link.wait_send()

    def pieces(self, wide, spread, source):
        plan = self.plan
        size = plan.h * plan.wp
        (block, cols, rows), _ = self.tm[source]

        def of(value, border, side):
            out = []
            for f in range(plan.f):
                top = border[pl.ds(f * plan.wp, plan.wp)].astype(F32)
                low = border[pl.ds((plan.f + f) * plan.wp, plan.wp)].astype(F32)
                out.append((side, top, value[f * size : (f + 1) * size], low))
            return out

        inner = of(wide[...] + spread_cols(self.cols_in, spread), self.rows_in, None)
        outer = of(block[...].astype(F32) + spread_cols(cols, spread), rows, source)
        if source == "past":
            return outer[plan.f - 2 :] + inner
        return inner + outer[:2]


def spread_cols(cols, spread):
    return jnp.dot(spread[...], cols[...], preferred_element_type=F32)


def silu(v):
    return v / (1.0 + jnp.exp(-v))


def slope(v):
    sigm = 1.0 / (1.0 + jnp.exp(-v))
    return sigm * (1.0 + v * (1.0 - sigm))


def valid(plan, place, count, side, border):
    has = place.has
    w = lax.broadcasted_iota(jnp.int32, (count, plan.c), 0) & (plan.wp - 1)
    one = lambda cond: cond.astype(jnp.int32)
    mask = jnp.where(
        w < plan.w,
        1,
        jnp.where(
            w == plan.w,
            one(has["right"]),
            jnp.where(w == plan.wp - 1, one(has["left"]), 0),
        ),
    )
    for name in (side, border):
        if name is not None:
            mask = mask * one(has[name])
    return mask > 0


def store_shifted(plan, ref, at, value):
    count = value.shape[0]
    rows = value.reshape(count // plan.wp, plan.wp, plan.c)
    before = pltpu.roll(rows, 1, axis=1).reshape(value.shape)
    after = pltpu.roll(rows, plan.wp - 1, axis=1).reshape(value.shape)
    c = plan.c
    ref[pl.ds(at, count), 0:c] = before.astype(BF16)
    ref[pl.ds(at, count), c : 2 * c] = value.astype(BF16)
    ref[pl.ds(at, count), 2 * c : 3 * c] = after.astype(BF16)


def build(plan, ref, frames):
    for k, (top, rows, low) in enumerate(frames):
        at = k * plan.hp * plan.wp
        store_shifted(plan, ref, at, top)
        store_shifted(plan, ref, at + plan.wp, rows)
        store_shifted(plan, ref, at + (plan.h + 1) * plan.wp, low)


def convolve(plan, ref, kernel, out):
    size = plan.h * plan.wp

    def frame(f, carry):
        pieces = []
        for p in range(3):
            for q in range(3):
                at = pl.multiple_of(((f + p) * plan.hp + q) * plan.wp, plan.wp)
                pieces.append(ref[pl.ds(at, size), :])
        wide = jnp.dot(jnp.concatenate(pieces, axis=1), kernel[...], preferred_element_type=F32)
        w = lax.broadcasted_iota(jnp.int32, wide.shape, 0) & (plan.wp - 1)
        out[pl.ds(pl.multiple_of(f * size, size), size), :] = jnp.where(w < plan.w, wide, 0.0)
        return carry

    lax.fori_loop(0, plan.f, frame, 0)


def kernel_term(plan, ref, grad, part):
    size = plan.h * plan.wp
    turned = grad.T.astype(BF16)

    def tap(pq, carry):
        p, q = lax.div(pq, 3), lax.rem(pq, 3)
        pieces = []
        for f in range(plan.f):
            at = pl.multiple_of(((f + p) * plan.hp + q) * plan.wp, plan.wp)
            pieces.append(ref[pl.ds(at, size), :])
        term = jnp.dot(turned, jnp.concatenate(pieces, axis=0), preferred_element_type=F32)
        part[pl.ds(pl.multiple_of(pq * 3 * plan.c, 3 * plan.c), 3 * plan.c), :] = term.T
        return carry

    lax.fori_loop(0, 9, tap, 0)


def turn_kernel(plan, kernel, out):
    taps, c = 27, plan.c

    def tap(k, carry):
        source = kernel[pl.ds(pl.multiple_of((taps - 1 - k) * c, c), c), :]
        out[pl.ds(pl.multiple_of(k * c, c), c), :] = source.astype(F32).T.astype(BF16)
        return carry

    lax.fori_loop(0, taps, tap, 0)


def spaced(plan, ref, wide):
    wide[...] = jnp.zeros_like(wide)
    for f in range(plan.f):
        for y in range(plan.h):
            wide[pl.ds((f * plan.h + y) * plan.wp, plan.w)] = ref[f, y].astype(F32)


def unspaced(plan, value, ref):
    for f in range(plan.f):
        for y in range(plan.h):
            at = (f * plan.h + y) * plan.wp
            ref[f, y] = value[at : at + plan.w].astype(BF16)


def column_sum(value):
    return jnp.sum(value, axis=0, keepdims=True)


def body(plan, n_ex, *refs):
    refs = list(refs)
    take = lambda k: [refs.pop(0) for _ in range(k)]
    features, cotangent, kernel_one, kernel_two, norms = take(5)
    block_out, grad_input, part_one, part_two = take(4)
    wide_x, wide_g, wide_h, wide_l, wide_b = take(5)
    pick, spread, turned_one, turned_two = take(4)
    x3_one, x3_two, x3_g, x3_h = take(4)
    exchange_refs = [take(k) for k in n_ex]
    reduce_refs = [take(4) for _ in range(4)]
    sems = take(2)

    place = Place(plan)
    rows, others = place.partners(plan)
    per_reduce = len(rows) + len(others)
    exchanges = [
        Exchange(plan, place, r, sems, EX_SEMS * k, d)
        for k, (r, d) in enumerate(
            zip(exchange_refs, (("past",), ("future",), ("past", "future"), ("future",)))
        )
    ]
    ex_x, ex_g, ex_h, ex_l = exchanges
    reduces = [
        Reduce(plan, place, r, sems, EX_SEMS * 4 + per_reduce * k)
        for k, r in enumerate(reduce_refs)
    ]
    for ex in exchanges:
        ex.clear()

    barrier = pltpu.get_barrier_semaphore()
    for dev in rows + others:
        pl.semaphore_signal(barrier, inc=1, device_id=dev, device_id_type=MESH)

    c = plan.c
    per_group = c // GROUPS
    members = float(plan.f * plan.h * plan.w * plan.ntm * plan.nrow * plan.ncol * per_group)
    lane_i = lax.broadcasted_iota(jnp.int32, (c, c), 0)
    lane_j = lax.broadcasted_iota(jnp.int32, (c, c), 1)
    same = (lax.div(lane_i, per_group) == lax.div(lane_j, per_group)).astype(F32)

    def group_means(total):
        sums = jnp.dot(
            total, same, preferred_element_type=F32, precision=lax.Precision.HIGHEST
        )
        return sums[0:1] / members, sums[1:2] / members

    def moments(total):
        average, square = group_means(total)
        return average, lax.rsqrt(square - average * average + EPSILON)

    spaced(plan, features, wide_x)
    j = lax.broadcasted_iota(jnp.int32, (2 * plan.cb, plan.n), 0)
    at = lax.broadcasted_iota(jnp.int32, (2 * plan.cb, plan.n), 1)
    first = j < plan.cb
    pick[...] = (
        at == jnp.where(first, j * plan.wp, (j - plan.cb) * plan.wp + plan.w - 1)
    ).astype(F32).astype(BF16)
    at = lax.broadcasted_iota(jnp.int32, (plan.n, 2 * plan.cb), 0)
    j = lax.broadcasted_iota(jnp.int32, (plan.n, 2 * plan.cb), 1)
    first = j < plan.cb
    spread[...] = (
        at == jnp.where(first, j * plan.wp + plan.w, (j - plan.cb) * plan.wp + plan.wp - 1)
    ).astype(F32).astype(BF16)

    pl.semaphore_wait(barrier, per_reduce)
    gain_one, shift_one = norms[0:1], norms[1:2]
    gain_two, shift_two = norms[2:3], norms[3:4]

    x = wide_x[...]
    reduces[0].start(column_sum(x), column_sum(x * x))
    ex_x.start(wide_x, pick)
    spaced(plan, cotangent, wide_g)
    ex_g.start(wide_g, pick)
    reduces[0].middle()
    ex_x.middle(wide_x, spread)
    ex_g.middle(wide_g, spread)
    turn_kernel(plan, kernel_two, turned_two)
    ex_x.later()
    ex_g.later()
    turn_kernel(plan, kernel_one, turned_one)
    mean_one, scale_one = moments(reduces[0].finish())
    ex_x.finish()

    def unit_one(v):
        return (v - mean_one) * scale_one

    def frames_of(pieces, fn):
        out = []
        for side, top, rows_, low in pieces:
            keep = lambda v, border: jnp.where(
                valid(plan, place, v.shape[0], side, border), fn(v), 0.0
            )
            out.append((keep(top, "up"), keep(rows_, None), keep(low, "down")))
        return out

    build(
        plan,
        x3_one,
        frames_of(
            ex_x.pieces(wide_x, spread, "past"),
            lambda v: silu(unit_one(v) * gain_one + shift_one),
        ),
    )
    convolve(plan, x3_one, kernel_one, wide_h)
    hidden = wide_h[...]
    reduces[1].start(column_sum(hidden), column_sum(hidden * hidden))
    ex_h.start(wide_h, pick)
    reduces[1].middle()
    ex_h.middle(wide_h, spread)
    ex_g.finish()
    build(plan, x3_g, [p[1:] for p in ex_g.pieces(wide_g, spread, "future")])
    ex_h.later()
    convolve(plan, x3_g, turned_two, wide_b)
    mean_two, scale_two = moments(reduces[1].finish())

    def unit_two(v):
        return (v - mean_two) * scale_two

    unit = unit_two(wide_h[...])
    lifted = wide_b[...] * slope(unit * gain_two + shift_two) * gain_two
    wide_l[...] = lifted
    reduces[2].start(column_sum(lifted), column_sum(lifted * unit))
    ex_l.start(wide_l, pick)
    reduces[2].middle()
    ex_l.middle(wide_l, spread)
    ex_h.finish()
    build(
        plan,
        x3_two,
        frames_of(
            ex_h.pieces(wide_h, spread, "past"),
            lambda v: silu(unit_two(v) * gain_two + shift_two),
        ),
    )
    ex_l.later()
    kernel_term(plan, x3_two, wide_g[...], part_two)
    convolve(plan, x3_two, kernel_two, wide_b)
    unspaced(plan, wide_x[...] + wide_b[...], block_out)

    a_two, b_two = group_means(reduces[2].finish())
    ex_l.finish()
    frames = []
    for (side, *lifts), (_, *hids) in zip(
        ex_l.pieces(wide_l, spread, "future"), ex_h.pieces(wide_h, spread, "future")
    ):
        out = []
        for border, lift, hid in zip(("up", None, "down"), lifts, hids):
            value = scale_two * (lift - a_two - unit_two(hid) * b_two)
            out.append(jnp.where(valid(plan, place, lift.shape[0], side, border), value, 0.0))
        frames.append(tuple(out))
    build(plan, x3_h, frames)
    convolve(plan, x3_h, turned_one, wide_b)
    unit = unit_one(wide_x[...])
    lifted = wide_b[...] * slope(unit * gain_one + shift_one) * gain_one
    reduces[3].start(column_sum(lifted), column_sum(lifted * unit))
    wide_l[...] = lifted
    reduces[3].middle()
    w = lax.broadcasted_iota(jnp.int32, (plan.h * plan.wp, c), 0) & (plan.wp - 1)
    own = jnp.concatenate(
        [jnp.where(w < plan.w, frames[f][1], 0.0) for f in range(plan.f)], axis=0
    )
    kernel_term(plan, x3_one, own, part_one)
    a_one, b_one = group_means(reduces[3].finish())
    unit = unit_one(wide_x[...])
    unspaced(
        plan,
        wide_g[...] + scale_one * (wide_l[...] - a_one - unit * b_one),
        grad_input,
    )
    for item in exchanges + reduces:
        item.drain()


def block_kernel(plan, features, cotangent, kernel_one, kernel_two, norms):
    c, n = plan.c, plan.n
    half = plan.f * plan.wp
    exchange = []
    n_ex = []
    for count in (1, 1, 2, 1):
        shapes = [(n, c), (2 * plan.cb, c), (2 * plan.cb, c), (2 * half, c), (2 * half, c)]
        shapes += [(n, c), (2 * plan.cb, c), (2 * half, c)] * count
        n_ex.append(len(shapes))
        exchange += [pltpu.VMEM(s, BF16) for s in shapes]
    reduce = [
        pltpu.VMEM((8, c), F32),
        pltpu.VMEM((max(1, plan.na - 1), 8, c), F32),
        pltpu.VMEM((8, c), F32),
        pltpu.VMEM((max(1, plan.nb - 1), 8, c), F32),
    ] * 4
    sems = 4 * EX_SEMS + 4 * (plan.na + plan.nb - 2)
    vmem = pl.BlockSpec(memory_space=pltpu.VMEM)
    taps = kernel_one.shape[0]
    return pl.pallas_call(
        functools.partial(body, plan, n_ex),
        out_shape=(
            jax.ShapeDtypeStruct(features.shape, BF16),
            jax.ShapeDtypeStruct(features.shape, BF16),
            jax.ShapeDtypeStruct((taps, c), F32),
            jax.ShapeDtypeStruct((taps, c), F32),
        ),
        in_specs=[vmem] * 5,
        out_specs=(vmem,) * 4,
        scratch_shapes=[pltpu.VMEM((n, c), F32)] * 5
        + [pltpu.VMEM((2 * plan.cb, n), BF16), pltpu.VMEM((n, 2 * plan.cb), BF16)]
        + [pltpu.VMEM((taps, c), BF16)] * 2
        + [pltpu.VMEM((plan.np, 3 * c), BF16)] * 4
        + exchange
        + reduce
        + [pltpu.SemaphoreType.DMA((sems,))] * 2,
        compiler_params=pltpu.CompilerParams(
            collective_id=0, has_side_effects=True, vmem_limit_bytes=52 * 2**20
        ),
    )(features, cotangent, kernel_one, kernel_two, norms)


def local(features, cotangent, conv_one, conv_two, gain_one, shift_one, gain_two, shift_two):
    f, h, w, c = features.shape
    plan = Plan(f, h, w, c, tuple(lax.axis_size(a) for a in AXES))
    norms = jnp.stack([gain_one, shift_one, gain_two, shift_two])
    block_out, grad_input, part_one, part_two = block_kernel(
        plan, features, cotangent, conv_one.reshape(-1, c), conv_two.reshape(-1, c), norms
    )
    sum_one, sum_two = lax.psum((part_one, part_two), AXES)
    return block_out, grad_input, sum_one.reshape(conv_one.shape), sum_two.reshape(conv_two.shape)


def solution(mesh):
    block = P("tm", "row", "col", None)
    return jax.shard_map(
        local,
        mesh=mesh,
        in_specs=(block, block) + (P(),) * 6,
        out_specs=(block, block, P(), P()),
        check_vma=False,
    )
```

time: 462 us -> 216 us (0.47)
  blocking collectives: 165 us -> 0 us
  local copies, waits for them, and re-layouts: 98.6 us -> 8.97 us
  Pallas kernels: 0 us -> 55.1 us
  starting transfers between devices: 51.2 us -> 0.04 us
  waiting for transfers between devices: 87.2 us -> 137 us
  matrix products: 33 us -> 0 us
  other arithmetic: 10 us -> 0.72 us
    psum x4 -> x0, blocking collectives: 165 us -> none  [the longest x2 84.4 us: group_moments(): lax.psum((jnp.sum(grouped, axis=(0, 2)), jnp.sum(grouped * grouped, axis=...]
    pallas_call x0 -> x1, Pallas kernels: none -> 55.1 us  [block_kernel(): pl.pallas_call(functools.partial(body, plan, n_ex), out_shape=(jax.ShapeD...]
    ppermute x20 -> x0, starting transfers between devices: 51.2 us -> none  [the longest x8 29.5 us: with_halo(): lax.ppermute(lax.slice_in_dim(block, block.shape[dim] - width, None, axis...]
    psum x1, waiting for transfers between devices: 87 us -> 137 us  [local(): sum_one, sum_two = lax.psum((part_one, part_two), AXES)]
    unnamed x127 -> x10, local copies, waits for them, and re-layouts: 56.1 us -> 8.97 us
    dot_general x6 -> x0, matrix products: 33 us -> none  [the longest x2 16.2 us: kernel_term(): lax.dot_general(columns, gradient_flat, (((0,), (0,)), ((), ())), preferr...]
    dot_general x2 -> x0, local copies, waits for them, and re-layouts: 20.1 us -> none  [kernel_term(): lax.dot_general(columns, gradient_flat, (((0,), (0,)), ((), ())), preferr...]
    reshape x5 -> x0, local copies, waits for them, and re-layouts: 17.3 us -> none  [the longest x2 16.5 us: unfold_taps(): return stacked.reshape(frames * height * width, stacked.shape[3])]
  transfers between devices with their start and end apart: 21 -> 1, of which waited for: 3 -> 1; matrix products, arithmetic and copies ran while one was open for 25% -> 1% of each run, Pallas kernels for 0% -> 0%
where the time goes in v1:
time: 216 us
  waiting for transfers between devices  137 us (63%)
  Pallas kernels  55.1 us (26%)
  between operations  14 us (6%)
  local copies, waits for them, and re-layouts  8.97 us (4%)
    psum x1, waiting for transfers between devices, local(): sum_one, sum_two = lax.psum((part_one, part_two), AXES)  137 us
    pallas_call x1, Pallas kernels, block_kernel(): pl.pallas_call(functools.partial(body, plan, n_ex), out_shape=(jax.ShapeD...  55.1 us
    unnamed x10, local copies, waits for them, and re-layouts  8.97 us
  transfers between devices with their start and end apart: 1, of which 1 were waited for; matrix products, arithmetic and copies ran while one was open for 1% of the time, Pallas kernels for 0%

profile of v1, /device:TPU:0, one launch (start us, length us, event | category | flops | bytes accessed | tf_op | source)
XLA Modules:
  0.0 215.9 jit_solution(15744883459143811715)
XLA Ops:
  7.2 0.0 all-reduce.3.cloned.1.call-start
  7.2 1.0 copy.12.refs_0_
  8.2 1.0 copy.13.refs_1_
  9.1 0.7 pad_maximum_fusion.refs_4_
  9.9 0.0 copy-start
  9.9 1.2 copy-done
  11.0 55.1 %shard_map.111 = (bf16[2,15,26,128]{3,2,1,0:T(8,128)(2,1)S(1)}, bf16[2,15,26,128]{3,2,1,0:T(8,128)(2,1)S(1)}, f32[3456,128]{1,0:T(8,128)}, f32[3456,128]{1,0:T(8,128)}) custom-call(bf16[2,15,26,128]{3,2,1,0:T(8,128)(2,1)S(1)} %copy.12.refs_0_, bf16[2,15,26,128]{3,2,1,0:T(8,128)(2,1)S(1)} %copy.13.refs_1_, bf16[3456,128]{1,0:T(8,128)(2,1)S(1)} %bitcast.8, ...), custom_call_target="tpu_custom_call" | custom-call | tf_op jit(solution)/shard_map/pallas_call | solution.py:566
  66.1 0.0 all-reduce.3.cloned.1.call-update
  66.1 0.8 copy.14
  67.0 0.8 copy.15
  67.8 137.1 %all-reduce.3.cloned.1.call-done = (f32[27,128,128]{2,1,0:T(8,128)}, f32[27,128,128]{2,1,0:T(8,128)}) async-done(((f32[27,128,128]{2,1,0:T(8,128)}, f32[27,128,128]{2,1,0:T(8,128)}), (f32[27,128,128]{2,1,0:T(8,128)}, f32[27,128,128]{2,1,0:T(8,128)})) %all-reduce.3.cloned.1.call-update) | async-done | bytes 3538960 | tf_op jit(solution)/shard_map/psum | solution.py:596
  204.9 0.0 copy-start.1
  204.9 3.0 %copy.20 = f32[27,128,128]{2,1,0:T(8,128)} copy(f32[27,128,128]{2,1,0:T(8,128)} %get-tuple-element.24) | data formatting | bytes 3538944
  207.9 0.0 copy-done.1
  207.9 1.2 copy.21
Async XLA Ops:
  7.2 197.7 %all-reduce.3.cloned.1.call-start = ((), (), s32[]{:S(2)}) async-start(), calls=%async_computation | async-start | bytes 7077888 | tf_op jit(solution)/shard_map/psum | solution.py:596
  9.9 1.2 copy-start
  204.9 3.0 %copy-start.1 = (f32[27,128,128]{2,1,0:T(8,128)S(1)}, f32[27,128,128]{2,1,0:T(8,128)}, u32[]{:S(2)}) copy-start(f32[27,128,128]{2,1,0:T(8,128)} %get-tuple-element.25) | copy-start | bytes 5308420
Sparse Core Ops, SparseCore 0:
  66.3 138.5 all-reduce.2

commit v2 on v1

--- a/solution.py
+++ b/solution.py
@@ -29,6 +29,24 @@
         self.ntm, self.nrow, self.ncol = sizes
         self.na = self.nrow
         self.nb = self.ntm * self.ncol
+        self.taps_rows = 27 * c
+        unit = 16 * self.ntm * self.nrow * self.ncol
+        units = -(-self.taps_rows // unit)
+        first = -(-units // 2)
+        self.sum_rows = units * unit
+        self.parts = [(0, first * unit)]
+        if units > first:
+            self.parts.append((first * unit, (units - first) * unit))
+
+    def stages(self, order):
+        near = 2 if self.ncol % 2 == 0 else 1
+        known = dict(
+            near=("col", 1, near, True),
+            col=("col", near, self.ncol // near, False),
+            tm=("tm", 1, self.ntm, False),
+            row=("row", 1, self.nrow, True),
+        )
+        return [known[name] for name in order if known[name][2] > 1]
 
 
 class Link:
@@ -142,6 +160,115 @@
     def drain(self):
         for link in self.a + self.b:
             link.wait_send()
+
+
+class KernelSum:
+    def __init__(self, plan, place, stages, span, acc, done, outs, ins, sems, base):
+        self.acc, self.done, self.outs, self.ins = acc, done, outs, ins
+        self.stages = stages
+        at, count = span
+        self.spans, self.reduce, self.gather = [], [], []
+        for k, (axis, stride, ways, wide) in enumerate(stages):
+            here = dict(tm=place.t, row=place.r, col=place.c)[axis]
+            mine = lax.rem(lax.div(here, stride), ways)
+            piece = count // ways
+            aligned = lambda v: pl.multiple_of(v, 16)
+            kept = aligned(at + mine * piece)
+            links, sources = [], []
+            for d in range(1, ways):
+                other = lax.rem(mine + d, ways)
+                dev = {axis: here + (other - mine) * stride}
+                sent = aligned(at + other * piece)
+                if wide:
+                    src = acc.at[pl.ds(sent, piece)]
+                else:
+                    src = outs[k].at[d - 1]
+                    sources.append((d - 1, sent))
+                links.append((Link(src, ins[k].at[d - 1], sems, base, dev, None, None), dev))
+                base += 1
+            self.reduce.append([link for link, _ in links])
+            gathers = []
+            for _, dev in links:
+                part = done.at[pl.ds(kept, piece)]
+                gathers.append(Link(part, part, sems, base, dev, None, None))
+                base += 1
+            self.gather.append(gathers)
+            self.spans.append((kept, piece, sources))
+            at, count = kept, piece
+        self.base = base
+
+    def steps(self):
+        out = []
+        last = len(self.stages) - 1
+        for k in range(len(self.stages)):
+            out.append(functools.partial(self.reduce_step, k))
+        for k in range(last, -1, -1):
+            out.append(functools.partial(self.gather_step, k))
+        out.append(self.last_step)
+        return out
+
+    def reduce_step(self, k):
+        if k:
+            self.settle(k - 1)
+        kept, piece, sources = self.spans[k]
+        for slot, sent in sources:
+            self.outs[k][slot] = self.acc[pl.ds(sent, piece)].astype(BF16)
+        for link in self.reduce[k]:
+            link.start()
+
+    def settle(self, k):
+        kept, piece, _ = self.spans[k]
+        for link in self.reduce[k]:
+            link.wait_recv()
+        total = self.acc[pl.ds(kept, piece)]
+        for d in range(len(self.reduce[k])):
+            total = total + self.ins[k][d].astype(F32)
+        if k == len(self.stages) - 1:
+            self.done[pl.ds(kept, piece)] = total.astype(BF16)
+        else:
+            self.acc[pl.ds(kept, piece)] = total
+
+    def gather_step(self, k):
+        if k == len(self.stages) - 1:
+            self.settle(k)
+        else:
+            for link in self.gather[k + 1]:
+                link.wait_recv()
+        for link in self.gather[k]:
+            link.start()
+
+    def last_step(self):
+        for link in self.gather[0]:
+            link.wait_recv()
+
+    def drain(self):
+        for links in self.reduce + self.gather:
+            for link in links:
+                link.wait_send()
+
+
+ORDERS = (("near", "col", "tm", "row"), ("near", "tm", "col", "row"))
+
+
+def sum_scratch(plan):
+    shapes, counts = [], []
+    for order, (_, count) in zip(ORDERS, plan.parts):
+        outs, ins = [], []
+        for axis, stride, ways, wide in plan.stages(order):
+            piece = count // ways
+            shape = (ways - 1, piece, plan.c)
+            outs.append(pltpu.VMEM((1, 16, plan.c) if wide else shape, BF16))
+            ins.append(pltpu.VMEM(shape, F32 if wide else BF16))
+            count = piece
+        counts.append(len(outs))
+        shapes += outs + ins
+    return shapes, counts
+
+
+def sum_sems(plan):
+    return 2 * sum(
+        stage[2] - 1 for order, _ in zip(ORDERS, plan.parts) for stage in plan.stages(order)
+    )
 
 
 EX_SEMS = 10
@@ -208,7 +335,6 @@
             link.wait_recv()
         for source in self.directions:
             self.tm[source][1][1].start()
-        self.wide_ext = wide
         ends = spread_cols(self.cols_in, spread)
         size = plan.h * plan.wp
         for f in range(plan.f):
@@ -325,9 +451,8 @@
     lax.fori_loop(0, plan.f, frame, 0)
 
 
-def kernel_term(plan, ref, grad, part):
+def kernel_term(plan, ref, turned, part, low, high):
     size = plan.h * plan.wp
-    turned = grad.T.astype(BF16)
 
     def tap(pq, carry):
         p, q = lax.div(pq, 3), lax.rem(pq, 3)
@@ -339,7 +464,7 @@
         part[pl.ds(pl.multiple_of(pq * 3 * plan.c, 3 * plan.c), 3 * plan.c), :] = term.T
         return carry
 
-    lax.fori_loop(0, 9, tap, 0)
+    lax.fori_loop(low, high, tap, 0)
 
 
 def turn_kernel(plan, kernel, out):
@@ -381,6 +506,11 @@
     x3_one, x3_two, x3_g, x3_h = take(4)
     exchange_refs = [take(k) for k in n_ex]
     reduce_refs = [take(4) for _ in range(4)]
+    acc_one, acc_two, done_one, done_two = take(4)
+    sum_refs = []
+    for _ in range(2):
+        for count in sum_scratch(plan)[1]:
+            sum_refs.append((take(count), take(count)))
     sems = take(2)
 
     place = Place(plan)
@@ -397,6 +527,26 @@
         Reduce(plan, place, r, sems, EX_SEMS * 4 + per_reduce * k)
         for k, r in enumerate(reduce_refs)
     ]
+    sums = []
+    base = EX_SEMS * 4 + per_reduce * 4
+    for acc, done in ((acc_two, done_two), (acc_one, done_one)):
+        for order, span in zip(ORDERS, plan.parts):
+            outs, ins = sum_refs[len(sums)]
+            sums.append(
+                KernelSum(plan, place, plan.stages(order), span, acc, done, outs, ins, sems, base)
+            )
+            base = sums[-1].base
+        acc[pl.ds(plan.taps_rows, plan.sum_rows - plan.taps_rows)] = jnp.zeros(
+            (plan.sum_rows - plan.taps_rows, plan.c), F32
+        )
+    sums_two, sums_one = sums[: len(plan.parts)], sums[len(plan.parts) :]
+    steps_two = [list(group) for group in zip(*[item.steps() for item in sums_two])]
+
+    def advance():
+        if steps_two:
+            for step in steps_two.pop(0):
+                step()
+
     for ex in exchanges:
         ex.clear()
 
@@ -506,11 +656,9 @@
         ),
     )
     ex_l.later()
-    kernel_term(plan, x3_two, wide_g[...], part_two)
-    convolve(plan, x3_two, kernel_two, wide_b)
-    unspaced(plan, wide_x[...] + wide_b[...], block_out)
-
+    kernel_term(plan, x3_two, wide_g[...].T.astype(BF16), acc_two, 0, 9)
     a_two, b_two = group_means(reduces[2].finish())
+    advance()
     ex_l.finish()
     frames = []
     for (side, *lifts), (_, *hids) in zip(
@@ -522,17 +670,32 @@
             out.append(jnp.where(valid(plan, place, lift.shape[0], side, border), value, 0.0))
         frames.append(tuple(out))
     build(plan, x3_h, frames)
+    advance()
     convolve(plan, x3_h, turned_one, wide_b)
     unit = unit_one(wide_x[...])
     lifted = wide_b[...] * slope(unit * gain_one + shift_one) * gain_one
     reduces[3].start(column_sum(lifted), column_sum(lifted * unit))
     wide_l[...] = lifted
+    advance()
     reduces[3].middle()
     w = lax.broadcasted_iota(jnp.int32, (plan.h * plan.wp, c), 0) & (plan.wp - 1)
     own = jnp.concatenate(
         [jnp.where(w < plan.w, frames[f][1], 0.0) for f in range(plan.f)], axis=0
     )
-    kernel_term(plan, x3_one, own, part_one)
+    turned = own.T.astype(BF16)
+    ready = min(9, -(-plan.parts[0][1] // (3 * c)))
+    kernel_term(plan, x3_one, turned, acc_one, 0, ready)
+    steps_one = [item.steps() for item in sums_one]
+    steps_one[0].pop(0)()
+    advance()
+    kernel_term(plan, x3_one, turned, acc_one, ready, 9)
+    for steps in steps_one[1:]:
+        steps.pop(0)()
+    convolve(plan, x3_two, kernel_two, wide_b)
+    for steps in steps_one:
+        steps.pop(0)()
+    advance()
+    unspaced(plan, wide_x[...] + wide_b[...], block_out)
     a_one, b_one = group_means(reduces[3].finish())
     unit = unit_one(wide_x[...])
     unspaced(
@@ -540,7 +703,13 @@
         wide_g[...] + scale_one * (wide_l[...] - a_one - unit * b_one),
         grad_input,
     )
-    for item in exchanges + reduces:
+    while steps_one[0]:
+        for steps in steps_one:
+            steps.pop(0)()
+        advance()
+    part_two[...] = done_two[pl.ds(0, plan.taps_rows)]
+    part_one[...] = done_one[pl.ds(0, plan.taps_rows)]
+    for item in exchanges + reduces + sums:
         item.drain()
 
 
@@ -560,7 +729,7 @@
         pltpu.VMEM((8, c), F32),
         pltpu.VMEM((max(1, plan.nb - 1), 8, c), F32),
     ] * 4
-    sems = 4 * EX_SEMS + 4 * (plan.na + plan.nb - 2)
+    sems = 4 * EX_SEMS + 4 * (plan.na + plan.nb - 2) + 2 * sum_sems(plan)
     vmem = pl.BlockSpec(memory_space=pltpu.VMEM)
     taps = kernel_one.shape[0]
     return pl.pallas_call(
@@ -568,8 +737,8 @@
         out_shape=(
             jax.ShapeDtypeStruct(features.shape, BF16),
             jax.ShapeDtypeStruct(features.shape, BF16),
-            jax.ShapeDtypeStruct((taps, c), F32),
-            jax.ShapeDtypeStruct((taps, c), F32),
+            jax.ShapeDtypeStruct((taps, c), BF16),
+            jax.ShapeDtypeStruct((taps, c), BF16),
         ),
         in_specs=[vmem] * 5,
         out_specs=(vmem,) * 4,
@@ -579,6 +748,9 @@
         + [pltpu.VMEM((plan.np, 3 * c), BF16)] * 4
         + exchange
         + reduce
+        + [pltpu.VMEM((plan.sum_rows, c), F32)] * 2
+        + [pltpu.VMEM((plan.sum_rows, c), BF16)] * 2
+        + sum_scratch(plan)[0] * 2
         + [pltpu.SemaphoreType.DMA((sems,))] * 2,
         compiler_params=pltpu.CompilerParams(
             collective_id=0, has_side_effects=True, vmem_limit_bytes=52 * 2**20
@@ -593,8 +765,12 @@
     block_out, grad_input, part_one, part_two = block_kernel(
         plan, features, cotangent, conv_one.reshape(-1, c), conv_two.reshape(-1, c), norms
     )
-    sum_one, sum_two = lax.psum((part_one, part_two), AXES)
-    return block_out, grad_input, sum_one.reshape(conv_one.shape), sum_two.reshape(conv_two.shape)
+    return (
+        block_out,
+        grad_input,
+        part_one.astype(F32).reshape(conv_one.shape),
+        part_two.astype(F32).reshape(conv_two.shape),
+    )
 
 
 def solution(mesh):

time: 216 us -> 90.2 us (0.42)
  waiting for transfers between devices: 137 us -> 0 us
  Pallas kernels: 55.1 us -> 82 us
  between operations: 14 us -> 0.66 us
  local copies, waits for them, and re-layouts: 8.97 us -> 3.6 us
  other arithmetic: 0.72 us -> 3.54 us
    psum x1 -> x0, waiting for transfers between devices: 137 us -> none  [local(): sum_one, sum_two = lax.psum((part_one, part_two), AXES)]
    pallas_call x1, Pallas kernels: 55.1 us -> 82 us  [block_kernel(): pl.pallas_call(functools.partial(body, plan, n_ex), out_shape=(jax.ShapeD...]
    unnamed x10 -> x6, local copies, waits for them, and re-layouts: 8.97 us -> 3.6 us
    reshape x0 -> x2, other arithmetic: none -> 2.82 us  [the longest x1 1.41 us: local(): part_one.astype(F32).reshape(conv_one.shape)]
  transfers between devices with their start and end apart: 1 -> 0, of which waited for: 1 -> 0; matrix products, arithmetic and copies ran while one was open for 1% -> 0% of each run, Pallas kernels for 0% -> 0%
where the time goes in v2:
time: 90.2 us; the launch traced here: 89.8 us
  Pallas kernels  82 us (91%)
  local copies, waits for them, and re-layouts  3.6 us (4%)
  other arithmetic  3.54 us (4%)
    pallas_call x1, Pallas kernels, block_kernel(): pl.pallas_call(functools.partial(body, plan, n_ex), out_shape=(jax.ShapeD...  82 us
    unnamed x6, local copies, waits for them, and re-layouts  3.6 us

profile of v2, /device:TPU:0, one launch (start us, length us, event | category | flops | bytes accessed | tf_op | source)
XLA Modules:
  0.0 89.8 jit_solution(4403679319694622)
XLA Ops:
  0.6 0.7 pad_maximum_fusion.refs_4_
  1.3 1.0 %copy.12.refs_0_ = bf16[2,15,26,128]{3,2,1,0:T(8,128)(2,1)S(1)} copy(bf16[2,15,26,128]{3,0,2,1:T(2,128)(2,1)} %param.8) | data formatting | bytes 399360 | tf_op args[0]
  2.3 1.0 %copy.13.refs_1_ = bf16[2,15,26,128]{3,2,1,0:T(8,128)(2,1)S(1)} copy(bf16[2,15,26,128]{3,0,2,1:T(2,128)(2,1)} %param.9) | data formatting | bytes 399360 | tf_op args[1]
  3.3 82.0 %shard_map.111 = (bf16[2,15,26,128]{3,2,1,0:T(8,128)(2,1)S(1)}, bf16[2,15,26,128]{3,2,1,0:T(8,128)(2,1)S(1)}, bf16[3456,128]{1,0:T(8,128)(2,1)S(1)}, bf16[3456,128]{1,0:T(8,128)(2,1)}) custom-call(bf16[2,15,26,128]{3,2,1,0:T(8,128)(2,1)S(1)} %copy.12.refs_0_, bf16[2,15,26,128]{3,2,1,0:T(8,128)(2,1)S(1)} %copy.13.refs_1_, bf16[3456,128]{1,0:T(8,128)(2,1)} %bitcast.11, ...), custom_call_target="tpu_custom_call" | custom-call | tf_op jit(solution)/shard_map/pallas_call | solution.py:735
  85.3 0.0 copy-start
  85.3 0.8 copy.14
  86.2 0.8 copy.15
  87.0 1.4 %convert.2 = f32[27,128,128]{2,1,0:T(8,128)} convert(bf16[27,128,128]{2,1,0:T(8,128)(2,1)S(1)} %bitcast.10) | non-fusion elementwise | flops 442368 | bytes 2654208 | tf_op jit(solution)/shard_map/reshape | solution.py:771
  88.4 0.0 copy-done
  88.4 1.4 %convert.3 = f32[27,128,128]{2,1,0:T(8,128)} convert(bf16[27,128,128]{2,1,0:T(8,128)(2,1)S(1)} %bitcast.13) | non-fusion elementwise | flops 442368 | bytes 2654208 | tf_op jit(solution)/shard_map/reshape | solution.py:772
Async XLA Ops:
  85.3 3.1 %copy-start = (bf16[3456,128]{1,0:T(8,128)(2,1)S(1)}, bf16[3456,128]{1,0:T(8,128)(2,1)}, u32[]{:S(2)}) copy-start(bf16[3456,128]{1,0:T(8,128)(2,1)} %get-tuple-element.11) | copy-start | bytes 2654212

commit v3 on v2

--- a/solution.py
+++ b/solution.py
@@ -499,7 +499,7 @@
 def body(plan, n_ex, *refs):
     refs = list(refs)
     take = lambda k: [refs.pop(0) for _ in range(k)]
-    features, cotangent, kernel_one, kernel_two, norms = take(5)
+    features, cotangent, kernel_one, kernel_two, *norms = take(8)
     block_out, grad_input, part_one, part_two = take(4)
     wide_x, wide_g, wide_h, wide_l, wide_b = take(5)
     pick, spread, turned_one, turned_two = take(4)
@@ -585,9 +585,9 @@
         at == jnp.where(first, j * plan.wp + plan.w, (j - plan.cb) * plan.wp + plan.wp - 1)
     ).astype(F32).astype(BF16)
 
+    turn_kernel(plan, kernel_two, turned_two)
     pl.semaphore_wait(barrier, per_reduce)
-    gain_one, shift_one = norms[0:1], norms[1:2]
-    gain_two, shift_two = norms[2:3], norms[3:4]
+    gain_one, shift_one, gain_two, shift_two = (ref[...] for ref in norms)
 
     x = wide_x[...]
     reduces[0].start(column_sum(x), column_sum(x * x))
@@ -597,7 +597,6 @@
     reduces[0].middle()
     ex_x.middle(wide_x, spread)
     ex_g.middle(wide_g, spread)
-    turn_kernel(plan, kernel_two, turned_two)
     ex_x.later()
     ex_g.later()
     turn_kernel(plan, kernel_one, turned_one)
@@ -671,13 +670,6 @@
         frames.append(tuple(out))
     build(plan, x3_h, frames)
     advance()
-    convolve(plan, x3_h, turned_one, wide_b)
-    unit = unit_one(wide_x[...])
-    lifted = wide_b[...] * slope(unit * gain_one + shift_one) * gain_one
-    reduces[3].start(column_sum(lifted), column_sum(lifted * unit))
-    wide_l[...] = lifted
-    advance()
-    reduces[3].middle()
     w = lax.broadcasted_iota(jnp.int32, (plan.h * plan.wp, c), 0) & (plan.wp - 1)
     own = jnp.concatenate(
         [jnp.where(w < plan.w, frames[f][1], 0.0) for f in range(plan.f)], axis=0
@@ -691,12 +683,26 @@
     kernel_term(plan, x3_one, turned, acc_one, ready, 9)
     for steps in steps_one[1:]:
         steps.pop(0)()
+
+    def advance_one():
+        for steps in steps_one:
+            steps.pop(0)()
+
+    convolve(plan, x3_h, turned_one, wide_b)
+    unit = unit_one(wide_x[...])
+    lifted = wide_b[...] * slope(unit * gain_one + shift_one) * gain_one
+    reduces[3].start(column_sum(lifted), column_sum(lifted * unit))
+    wide_l[...] = lifted
+    advance_one()
+    advance()
+    reduces[3].middle()
     convolve(plan, x3_two, kernel_two, wide_b)
-    for steps in steps_one:
-        steps.pop(0)()
+    advance_one()
     advance()
     unspaced(plan, wide_x[...] + wide_b[...], block_out)
     a_one, b_one = group_means(reduces[3].finish())
+    advance_one()
+    advance()
     unit = unit_one(wide_x[...])
     unspaced(
         plan,
@@ -704,8 +710,7 @@
         grad_input,
     )
     while steps_one[0]:
-        for steps in steps_one:
-            steps.pop(0)()
+        advance_one()
         advance()
     part_two[...] = done_two[pl.ds(0, plan.taps_rows)]
     part_one[...] = done_one[pl.ds(0, plan.taps_rows)]
@@ -713,7 +718,7 @@
         item.drain()
 
 
-def block_kernel(plan, features, cotangent, kernel_one, kernel_two, norms):
+def block_kernel(plan, features, cotangent, kernel_one, kernel_two, *norms):
     c, n = plan.c, plan.n
     half = plan.f * plan.wp
     exchange = []
@@ -740,7 +745,7 @@
             jax.ShapeDtypeStruct((taps, c), BF16),
             jax.ShapeDtypeStruct((taps, c), BF16),
         ),
-        in_specs=[vmem] * 5,
+        in_specs=[vmem] * 8,
         out_specs=(vmem,) * 4,
         scratch_shapes=[pltpu.VMEM((n, c), F32)] * 5
         + [pltpu.VMEM((2 * plan.cb, n), BF16), pltpu.VMEM((n, 2 * plan.cb), BF16)]
@@ -755,15 +760,15 @@
         compiler_params=pltpu.CompilerParams(
             collective_id=0, has_side_effects=True, vmem_limit_bytes=52 * 2**20
         ),
-    )(features, cotangent, kernel_one, kernel_two, norms)
+    )(features, cotangent, kernel_one, kernel_two, *norms)
 
 
 def local(features, cotangent, conv_one, conv_two, gain_one, shift_one, gain_two, shift_two):
     f, h, w, c = features.shape
     plan = Plan(f, h, w, c, tuple(lax.axis_size(a) for a in AXES))
-    norms = jnp.stack([gain_one, shift_one, gain_two, shift_two])
+    norms = [v.reshape(1, c) for v in (gain_one, shift_one, gain_two, shift_two)]
     block_out, grad_input, part_one, part_two = block_kernel(
-        plan, features, cotangent, conv_one.reshape(-1, c), conv_two.reshape(-1, c), norms
+        plan, features, cotangent, conv_one.reshape(-1, c), conv_two.reshape(-1, c), *norms
     )
     return (
         block_out,

time: 90.2 us -> 91.7 us (1.017)
  local copies, waits for them, and re-layouts: 3.6 us -> 6.22 us
    unnamed x6 -> x14, local copies, waits for them, and re-layouts: 3.6 us -> 6.22 us
where the time goes in v3:
time: 91.7 us; the launch traced here: 91.3 us
  Pallas kernels  81.6 us (89%)
  local copies, waits for them, and re-layouts  6.22 us (7%)
  other arithmetic  2.81 us (3%)
    pallas_call x1, Pallas kernels, block_kernel(): pl.pallas_call(functools.partial(body, plan, n_ex), out_shape=(jax.ShapeD...  81.6 us
    unnamed x14, local copies, waits for them, and re-layouts  6.22 us

profile of v3, /device:TPU:0, one launch (start us, length us, event | category | flops | bytes accessed | tf_op | source)
XLA Modules:
  0.0 91.3 jit_solution(2702050584245738702)
XLA Ops:
  0.6 1.0 %copy.12.refs_0_ = bf16[2,15,26,128]{3,2,1,0:T(8,128)(2,1)S(1)} copy(bf16[2,15,26,128]{3,0,2,1:T(2,128)(2,1)} %param.8) | data formatting | bytes 399360 | tf_op args[0]
  1.6 1.0 %copy.13.refs_1_ = bf16[2,15,26,128]{3,2,1,0:T(8,128)(2,1)S(1)} copy(bf16[2,15,26,128]{3,0,2,1:T(2,128)(2,1)} %param.9) | data formatting | bytes 399360 | tf_op args[1]
  2.6 0.0 copy-start
  2.6 0.6 copy-done
  3.2 0.0 copy-start.1
  3.2 0.7 copy-done.1
  3.9 0.0 copy-start.2
  3.9 0.7 copy-done.2
  4.5 0.0 copy-start.3
  4.5 0.7 copy-done.3
  5.2 81.6 %shard_map.111 = (bf16[2,15,26,128]{3,2,1,0:T(8,128)(2,1)S(1)}, bf16[2,15,26,128]{3,2,1,0:T(8,128)(2,1)S(1)}, bf16[3456,128]{1,0:T(8,128)(2,1)S(1)}, bf16[3456,128]{1,0:T(8,128)(2,1)}) custom-call(bf16[2,15,26,128]{3,2,1,0:T(8,128)(2,1)S(1)} %copy.12.refs_0_, bf16[2,15,26,128]{3,2,1,0:T(8,128)(2,1)S(1)} %copy.13.refs_1_, bf16[3456,128]{1,0:T(8,128)(2,1)} %bitcast.15, ...), custom_call_target="tpu_custom_call" | custom-call | tf_op jit(solution)/shard_map/pallas_call | solution.py:740
  86.8 0.0 copy-start.4
  86.8 0.8 copy.14
  87.7 0.8 copy.15
  88.5 1.4 %convert.2 = f32[27,128,128]{2,1,0:T(8,128)} convert(bf16[27,128,128]{2,1,0:T(8,128)(2,1)S(1)} %bitcast.10) | non-fusion elementwise | flops 442368 | bytes 2654208 | tf_op jit(solution)/shard_map/reshape | solution.py:776
  89.9 0.0 copy-done.4
  89.9 1.4 %convert.3 = f32[27,128,128]{2,1,0:T(8,128)} convert(bf16[27,128,128]{2,1,0:T(8,128)(2,1)S(1)} %bitcast.17) | non-fusion elementwise | flops 442368 | bytes 2654208 | tf_op jit(solution)/shard_map/reshape | solution.py:777
Async XLA Ops:
  2.6 0.7 copy-start
  3.2 0.7 copy-start.1
  3.9 0.7 copy-start.2
  4.5 0.7 copy-start.3
  86.8 3.1 %copy-start.4 = (bf16[3456,128]{1,0:T(8,128)(2,1)S(1)}, bf16[3456,128]{1,0:T(8,128)(2,1)}, u32[]{:S(2)}) copy-start(bf16[3456,128]{1,0:T(8,128)(2,1)} %get-tuple-element.11) | copy-start | bytes 2654212

commit v4 on v3

--- a/solution.py
+++ b/solution.py
@@ -44,7 +44,7 @@
             near=("col", 1, near, True),
             col=("col", near, self.ncol // near, False),
             tm=("tm", 1, self.ntm, False),
-            row=("row", 1, self.nrow, True),
+            row=("row", 1, self.nrow, False),
         )
         return [known[name] for name in order if known[name][2] > 1]
 
@@ -585,7 +585,6 @@
         at == jnp.where(first, j * plan.wp + plan.w, (j - plan.cb) * plan.wp + plan.wp - 1)
     ).astype(F32).astype(BF16)
 
-    turn_kernel(plan, kernel_two, turned_two)
     pl.semaphore_wait(barrier, per_reduce)
     gain_one, shift_one, gain_two, shift_two = (ref[...] for ref in norms)
 
@@ -597,6 +596,7 @@
     reduces[0].middle()
     ex_x.middle(wide_x, spread)
     ex_g.middle(wide_g, spread)
+    turn_kernel(plan, kernel_two, turned_two)
     ex_x.later()
     ex_g.later()
     turn_kernel(plan, kernel_one, turned_one)

time: 91.7 us -> 88.2 us (0.962)
  Pallas kernels: 81.6 us -> 78.1 us
    pallas_call x1, Pallas kernels: 81.6 us -> 78.1 us  [block_kernel(): pl.pallas_call(functools.partial(body, plan, n_ex), out_shape=(jax.ShapeD...]
where the time goes in v4:
time: 88.2 us; the launch traced here: 87.8 us
  Pallas kernels  78.1 us (89%)
  local copies, waits for them, and re-layouts  6.22 us (7%)
  other arithmetic  2.81 us (3%)
    pallas_call x1, Pallas kernels, block_kernel(): pl.pallas_call(functools.partial(body, plan, n_ex), out_shape=(jax.ShapeD...  78.1 us
    unnamed x14, local copies, waits for them, and re-layouts  6.22 us

profile of v4, /device:TPU:0, one launch (start us, length us, event | category | flops | bytes accessed | tf_op | source)
XLA Modules:
  0.0 87.8 jit_solution(14320682873756750544)
XLA Ops:
  0.6 1.0 %copy.12.refs_0_ = bf16[2,15,26,128]{3,2,1,0:T(8,128)(2,1)S(1)} copy(bf16[2,15,26,128]{3,0,2,1:T(2,128)(2,1)} %param.8) | data formatting | bytes 399360 | tf_op args[0]
  1.6 1.0 %copy.13.refs_1_ = bf16[2,15,26,128]{3,2,1,0:T(8,128)(2,1)S(1)} copy(bf16[2,15,26,128]{3,0,2,1:T(2,128)(2,1)} %param.9) | data formatting | bytes 399360 | tf_op args[1]
  2.6 0.0 copy-start
  2.6 0.6 copy-done
  3.2 0.0 copy-start.1
  3.2 0.7 copy-done.1
  3.9 0.0 copy-start.2
  3.9 0.7 copy-done.2
  4.5 0.0 copy-start.3
  4.5 0.7 copy-done.3
  5.2 78.1 %shard_map.111 = (bf16[2,15,26,128]{3,2,1,0:T(8,128)(2,1)S(1)}, bf16[2,15,26,128]{3,2,1,0:T(8,128)(2,1)S(1)}, bf16[3456,128]{1,0:T(8,128)(2,1)S(1)}, bf16[3456,128]{1,0:T(8,128)(2,1)}) custom-call(bf16[2,15,26,128]{3,2,1,0:T(8,128)(2,1)S(1)} %copy.12.refs_0_, bf16[2,15,26,128]{3,2,1,0:T(8,128)(2,1)S(1)} %copy.13.refs_1_, bf16[3456,128]{1,0:T(8,128)(2,1)} %bitcast.15, ...), custom_call_target="tpu_custom_call" | custom-call | tf_op jit(solution)/shard_map/pallas_call | solution.py:740
  83.3 0.0 copy-start.4
  83.3 0.8 copy.14
  84.1 0.8 copy.15
  85.0 1.4 %convert.2 = f32[27,128,128]{2,1,0:T(8,128)} convert(bf16[27,128,128]{2,1,0:T(8,128)(2,1)S(1)} %bitcast.10) | non-fusion elementwise | flops 442368 | bytes 2654208 | tf_op jit(solution)/shard_map/reshape | solution.py:776
  86.4 0.0 copy-done.4
  86.4 1.4 %convert.3 = f32[27,128,128]{2,1,0:T(8,128)} convert(bf16[27,128,128]{2,1,0:T(8,128)(2,1)S(1)} %bitcast.17) | non-fusion elementwise | flops 442368 | bytes 2654208 | tf_op jit(solution)/shard_map/reshape | solution.py:777
Async XLA Ops:
  2.6 0.7 copy-start
  3.2 0.7 copy-start.1
  3.9 0.7 copy-start.2
  4.5 0.7 copy-start.3
  83.3 3.1 %copy-start.4 = (bf16[3456,128]{1,0:T(8,128)(2,1)S(1)}, bf16[3456,128]{1,0:T(8,128)(2,1)}, u32[]{:S(2)}) copy-start(bf16[3456,128]{1,0:T(8,128)(2,1)} %get-tuple-element.11) | copy-start | bytes 2654212
